TPU v7x, 128 devices: a whole 4x4x4 slice. The times are simulated.
128 devices in a mesh: group: 32 (over z, y, x_hi), head: 4 (over x_lo, core).
Axes of the slice: x: 4 (x_hi: 2, x_lo: 2; x = x_hi * 2 + x_lo), y: 4, z: 4, core: 2. Of those that a mesh axis runs over, the one named last changes fastest.
Arguments:
- tokens: bfloat16 [4, 4096, 1536], P(None, 'group'), may hold values from -6 to 6
- parents: int32 [3, 4096], P(None, 'group'), may hold values from 0 to 7
- page_request: int32 [1536], P('group'), may hold values from 0 to 511, as said below
- page_fill: int32 [1536], P('group'), may hold values from 1 to 128, as said below
- keys_pool: bfloat16 [1536, 1536, 128], P('group', 'head'), may hold values from -600 to 600
- values_pool: bfloat16 [1536, 1536, 128], P('group', 'head'), may hold values from -6 to 6
- decay_pool: bfloat16 [1536, 24, 128], P('group', 'head'), may hold values from -494.52 to 0
- gain_attn: float32 [1536], replicated, may hold values from 0.1 to 1.9
- w_query: bfloat16 [1536, 1536], P('head'), may hold values from -0.15625 to 0.15625
- w_key: bfloat16 [1536, 1536], P('head'), may hold values from -0.15625 to 0.15625
- w_value: bfloat16 [1536, 1536], P('head'), may hold values from -0.15625 to 0.15625
- w_forget: bfloat16 [1536, 24], P(None, 'head'), may hold values from -0.15625 to 0.15625
- forget_bias: float32 [24], P('head'), may hold values from -2 to 6
- w_out: bfloat16 [1536, 1536], P('head'), may hold values from -0.15625 to 0.15625
- gain_ffn: float32 [1536], replicated, may hold values from 0.1 to 1.9
- w_gate: bfloat16 [1536, 4096], P(None, 'head'), may hold values from -0.15625 to 0.15625
- w_up: bfloat16 [1536, 4096], P(None, 'head'), may hold values from -0.15625 to 0.15625
- w_down: bfloat16 [4096, 1536], P('head'), may hold values from -0.09375 to 0.09375
Outputs:
- outputs: bfloat16 [4, 4096, 1536], P(None, 'group')
Inputs may be any that keep to these rules, and one draw needn't show every extreme that they name: `page_request`: request ids g * 16 to g * 16 + 15 are the requests owned by group g, and pages g * 48 to g * 48 + 47 are the page slots of group g. The first 32 slots of a group hold pages of its own requests; its other 16 slots hold pages of other groups' requests, at most 1 from the requests of one group. Every request has at least one page. `page_fill`: the valid positions of a page are its first ones.
All inputs are finite; a program needn't handle non-finite values.
Results may differ from a plain program's by a relative error of at most 0.0095.
Values may be sent and summed in bfloat16 or wider, within the bound.
A program may use at most 192 MiB of HBM per device.

v0:
```python
import jax
import jax.numpy as jnp
from jax import lax
from jax.sharding import PartitionSpec as P

BEAMS = 8
OWNED_SLOTS = 32
SPILL = 16
epsilon = 1e-05
masked_score = -1e30


def rms_scale(values, gain_vector):
    widened = values.astype(jnp.float32)
    return (
        widened
        * lax.rsqrt(jnp.mean(widened * widened, axis=-1, keepdims=True) + epsilon)
        * gain_vector
    )


def page_partials(page_keys, page_values, page_decay, fill_count, asked_rows, head_count):
    page_count, inner_width, length = page_keys.shape
    head_size = inner_width // head_count
    keys_split = page_keys.reshape(page_count, head_count, head_size, length)
    values_split = page_values.reshape(page_count, head_count, head_size, length)
    asked_split = asked_rows.reshape(asked_rows.shape[:3] + (head_count, head_size))
    scores = jnp.einsum(
        "pbshd,phdt->pbsht", asked_split, keys_split, preferred_element_type=jnp.float32
    ) * head_size ** (-0.5)
    scores = scores + page_decay.astype(jnp.float32)[:, None, None, :, :]
    valid_mask = jnp.arange(length)[None, :] < fill_count[:, None]
    scores = jnp.where(valid_mask[:, None, None, None, :], scores, masked_score)
    page_top = jnp.max(scores, axis=-1)
    weights = jnp.exp(scores - page_top[..., None])
    page_total = jnp.sum(weights, axis=-1)
    numerator = jnp.einsum(
        "pbsht,phdt->pbshd",
        weights.astype(jnp.bfloat16),
        values_split,
        preferred_element_type=jnp.float32,
    )
    return (page_top, page_total, numerator.reshape(numerator.shape[:3] + (inner_width,)))


def by_request(current_request, page_top, page_total, numerator, request_count, head_count):
    matches = current_request[None, :] == jnp.arange(request_count)[:, None]
    wide_match = matches[:, :, None, None, None]
    best_top = jnp.max(jnp.where(wide_match, page_top[None], masked_score), axis=1)
    factor = jnp.where(wide_match, jnp.exp(page_top[None] - best_top[:, None]), 0.0)
    summed = jnp.sum(factor * page_total[None], axis=1)
    numer_split = numerator.reshape(numerator.shape[:3] + (head_count, -1))
    combined = jnp.sum(factor[..., None] * numer_split[None], axis=1)
    return (best_top, summed, combined.reshape(combined.shape[:3] + (-1,)))


def shards(
    tokens,
    parents,
    page_request,
    page_fill,
    keys_pool,
    values_pool,
    decay_pool,
    gain_attn,
    w_query,
    w_key,
    w_value,
    w_forget,
    forget_bias,
    w_out,
    gain_ffn,
    w_gate,
    w_up,
    w_down,
):
    step_count, row_count, model_width = tokens.shape
    head_count = w_forget.shape[1]
    inner_width = w_query.shape[0]
    head_size = inner_width // head_count
    local_count = row_count // BEAMS
    groups = lax.axis_size("group")
    own_group = lax.axis_index("group")
    capacity = (SPILL + groups - 2) // (groups - 1)
    flat_tokens = tokens.reshape(step_count * row_count, model_width)
    normed = rms_scale(flat_tokens, gain_attn).astype(jnp.bfloat16)

    def project(weight):
        product = lax.dot_general(
            normed, weight, (((1,), (1,)), ((), ())), preferred_element_type=jnp.float32
        )
        return product.astype(jnp.bfloat16).reshape(step_count, row_count, -1)

    queries = project(w_query)
    key_new = project(w_key)
    value_new = project(w_value)
    forget = jax.nn.log_sigmoid(
        jnp.dot(normed, w_forget, preferred_element_type=jnp.float32) + forget_bias
    ).reshape(step_count, row_count, head_count)
    by_row = queries.transpose(1, 0, 2)
    by_request_rows = by_row.reshape(local_count, BEAMS, step_count, inner_width)
    own_request = page_request[:OWNED_SLOTS] - own_group * local_count
    own_parts = page_partials(
        keys_pool[:OWNED_SLOTS],
        values_pool[:OWNED_SLOTS],
        decay_pool[:OWNED_SLOTS],
        page_fill[:OWNED_SLOTS],
        by_request_rows[own_request],
        head_count,
    )
    hosted_request = page_request[OWNED_SLOTS:]
    hosted_owner = hosted_request // local_count
    hosted_local = hosted_request % local_count
    hosted_index = jnp.arange(hosted_request.shape[0])
    earlier = (hosted_owner[:, None] == hosted_owner[None, :]) & (
        hosted_index[None, :] < hosted_index[:, None]
    )
    hosted_rank = jnp.sum(earlier, axis=1)
    slot_match = (hosted_owner[None, None, :] == jnp.arange(groups)[:, None, None]) & (
        hosted_rank[None, None, :] == jnp.arange(capacity)[None, :, None]
    )
    slot_full = jnp.any(slot_match, axis=2)
    slot_source = jnp.sum(jnp.where(slot_match, hosted_index[None, None, :], 0), axis=2)
    slot_local = jnp.sum(jnp.where(slot_match, hosted_local[None, None, :], 0), axis=2)
    slot_count = groups * capacity
    base_rows = jnp.arange(row_count) // BEAMS * BEAMS
    hist_keys = jnp.zeros((0, row_count, inner_width), jnp.bfloat16)
    hist_values = jnp.zeros((0, row_count, inner_width), jnp.bfloat16)
    hist_totals = jnp.zeros((0, row_count, head_count), jnp.float32)
    running = jnp.zeros((row_count, head_count), jnp.float32)
    finished = []
    for step_index in range(step_count):
        query_block = by_row[:, step_index : step_index + 1]
        step_span = query_block.shape[1]
        gathered = lax.all_gather(query_block, "group", axis=0, tiled=True)
        asked_rows = gathered.reshape(groups * local_count, BEAMS, step_span, inner_width)[
            hosted_request
        ]
        page_top, page_total, numerator = page_partials(
            keys_pool[OWNED_SLOTS:],
            values_pool[OWNED_SLOTS:],
            decay_pool[OWNED_SLOTS:],
            page_fill[OWNED_SLOTS:],
            asked_rows,
            head_count,
        )
        full_slot = slot_full[:, :, None, None, None]
        own_now = tuple((member[:, :, step_index : step_index + 1] for member in own_parts))
        all_request = jnp.concatenate(
            [
                own_request,
                lax.all_to_all(
                    slot_local.astype(jnp.float32), "group", split_axis=0, concat_axis=0, tiled=True
                )
                .reshape(slot_count)
                .astype(jnp.int32),
            ],
            axis=0,
        )
        all_top = jnp.concatenate(
            [
                own_now[0],
                lax.all_to_all(
                    jnp.where(full_slot, page_top[slot_source], masked_score),
                    "group",
                    split_axis=0,
                    concat_axis=0,
                    tiled=True,
                ).reshape((slot_count,) + page_top.shape[1:]),
            ],
            axis=0,
        )
        all_total = jnp.concatenate(
            [
                own_now[1],
                lax.all_to_all(
                    jnp.where(full_slot, page_total[slot_source], 0.0),
                    "group",
                    split_axis=0,
                    concat_axis=0,
                    tiled=True,
                ).reshape((slot_count,) + page_total.shape[1:]),
            ],
            axis=0,
        )
        all_numer = jnp.concatenate(
            [
                own_now[2],
                lax.all_to_all(
                    jnp.where(full_slot, numerator[slot_source], 0.0),
                    "group",
                    split_axis=0,
                    concat_axis=0,
                    tiled=True,
                ).reshape((slot_count,) + numerator.shape[1:]),
            ],
            axis=0,
        )
        page_top, page_total, page_numer = by_request(
            all_request, all_top, all_total, all_numer, local_count, head_count
        )
        page_top = page_top.reshape(row_count, head_count)
        page_total = page_total.reshape(row_count, head_count)
        page_numer = page_numer.reshape(row_count, head_count, head_size)
        if step_index > 0:
            source = base_rows + parents[step_index - 1]
            hist_keys = hist_keys[:, source]
            hist_values = hist_values[:, source]
            hist_totals = hist_totals[:, source]
            running = running[source]
        running = running + forget[step_index]
        hist_keys = jnp.concatenate([hist_keys, key_new[step_index][None]], axis=0)
        hist_values = jnp.concatenate([hist_values, value_new[step_index][None]], axis=0)
        hist_totals = jnp.concatenate([hist_totals, running[None]], axis=0)
        asked_now = queries[step_index].reshape(row_count, head_count, head_size)
        keys_now = hist_keys.reshape(step_index + 1, row_count, head_count, head_size)
        values_now = hist_values.reshape(step_index + 1, row_count, head_count, head_size)
        scores = jnp.einsum(
            "rhd,urhd->rhu", asked_now, keys_now, preferred_element_type=jnp.float32
        ) * head_size ** (-0.5) - hist_totals.transpose(1, 2, 0)
        history_top = jnp.max(scores, axis=-1)
        weights = jnp.exp(scores - history_top[..., None])
        history_total = jnp.sum(weights, axis=-1)
        history_numer = jnp.einsum(
            "rhu,urhd->rhd",
            weights.astype(jnp.bfloat16),
            values_now,
            preferred_element_type=jnp.float32,
        )
        best_top = jnp.maximum(page_top, history_top)
        page_scale = jnp.exp(page_top - best_top)
        history_scale = jnp.exp(history_top - best_top)
        total_sum = page_total * page_scale + history_total * history_scale
        numer_sum = page_numer * page_scale[..., None] + history_numer * history_scale[..., None]
        attended = (
            (numer_sum / total_sum[..., None]).astype(jnp.bfloat16).reshape(row_count, inner_width)
        )
        mixed_sum = lax.psum(jnp.dot(attended, w_out, preferred_element_type=jnp.float32), "head")
        residual = tokens[step_index].astype(jnp.float32) + mixed_sum
        normed_ffn = rms_scale(residual, gain_ffn).astype(jnp.bfloat16)
        gate_proj = jnp.dot(normed_ffn, w_gate, preferred_element_type=jnp.float32)
        up_proj = jnp.dot(normed_ffn, w_up, preferred_element_type=jnp.float32)
        hidden = (jax.nn.silu(gate_proj) * up_proj).astype(jnp.bfloat16)
        down_sum = lax.psum(jnp.dot(hidden, w_down, preferred_element_type=jnp.float32), "head")
        finished.append((residual + down_sum).astype(jnp.bfloat16))
    result = jnp.stack(finished, axis=0)
    return result


def solution(mesh):
    return jax.shard_map(
        shards,
        mesh=mesh,
        in_specs=(
            P(None, "group", None),
            P(None, "group"),
            P("group"),
            P("group"),
            P("group", "head", None),
            P("group", "head", None),
            P("group", "head", None),
            P(),
            P("head", None),
            P("head", None),
            P("head", None),
            P(None, "head"),
            P("head"),
            P("head", None),
            P(),
            P(None, "head"),
            P(None, "head"),
            P("head", None),
        ),
        out_specs=P(None, "group", None),
        check_vma=False,
    )
```

profile of v0, /device:TPU:1, one launch (start us, length us, event | category | flops | bytes accessed | tf_op | source)
XLA Modules:
  0.0 839.9 jit_solution(794505036848824269)
XLA Ops:
  19.0 11.5 %all-to-all-start = ((f32[32,1,1]{2,1,0:T(1,128)}), f32[32,1,1]{2,1,0:T(1,128)}, u32[]{:S(2)}, u32[]{:S(2)}) async-start(f32[32,1,1]{2,1,0:T(1,128)} %copy.715), calls=%async_computation | async-start | bytes 32768 | tf_op jit(solution)/shard_map/all_to_all | solution.py:152
  35.8 3.9 slice.193
  43.6 3.7 reshape.1148
  47.3 3.8 bitcast_reduce_fusion
  56.5 4.7 copy.728
  61.2 4.6 reshape.1155
  79.7 2.8 slice.202
  82.5 2.8 slice.198
  140.6 2.8 gather_fusion.23
  179.1 67.7 %all-gather.11.cloned.1.call-done = bf16[4096,1,384]{2,0,1:T(8,128)(2,1)} async-done(((bf16[128,1,384]{2,0,1:T(8,128)(2,1)}), bf16[4096,1,384]{2,0,1:T(8,128)(2,1)}) %all-gather.11.cloned.1.call-update) | async-done | bytes 3145744 | tf_op jit(solution)/shard_map/all_gather | solution.py:135
  254.5 3.3 fusion.162
  259.4 3.4 fusion.164
  270.3 3.3 convolution_bitcast_fusion.2
  277.1 46.8 %all-gather.5.cloned.1.call-done = bf16[4096,1,384]{2,0,1:T(8,128)(2,1)} async-done(((bf16[128,1,384]{2,0,1:T(8,128)(2,1)}), bf16[4096,1,384]{2,0,1:T(8,128)(2,1)}) %all-gather.5.cloned.1.call-update) | async-done | bytes 3145744 | tf_op jit(solution)/shard_map/all_gather | solution.py:135
  372.1 5.6 all-to-all-start.1
  377.7 3.2 convolution_bitcast_fusion.4
  400.3 9.2 %all-to-all-start.4 = ((f32[32,1,8,1,6]{2,3,4,1,0:T(1,128)}), f32[32,1,8,1,6]{2,3,4,1,0:T(1,128)S(1)}, u32[]{:S(2)}, u32[]{:S(2)}) async-start(f32[32,1,8,1,6]{2,3,4,1,0:T(1,128)} %copy.745), calls=%async_computation.4 | async-start | bytes 196608 | tf_op jit(solution)/shard_map/all_to_all | solution.py:163
  409.5 2.7 fusion.69
  418.4 8.4 all-to-all-start.7
  426.9 8.7 %all-to-all-done.7 = f32[32,1,8,1,6]{2,3,4,1,0:T(1,128)S(1)} async-done(((f32[32,1,8,1,6]{2,3,4,1,0:T(1,128)}), f32[32,1,8,1,6]{2,3,4,1,0:T(1,128)S(1)}, u32[]{:S(2)}, u32[]{:S(2)}) %all-to-all-start.7) | async-done | bytes 6176 | tf_op jit(solution)/shard_map/all_to_all | solution.py:163
  435.6 4.3 all-to-all-start.10
  441.5 6.9 all-to-all-done.10
  448.4 3.8 all-to-all-start.3
  453.8 7.3 all-to-all-done.3
  461.1 3.8 all-to-all-start.12
  465.9 8.0 all-to-all-done.12
  473.9 4.5 all-to-all-start.6
  481.4 5.9 all-to-all-done.6
  487.3 4.5 all-to-all-start.9
  503.8 9.2 %all-to-all-start.2 = ((f32[32,1,8,1,384]{4,2,3,1,0:T(8,128)}), f32[32,1,8,1,384]{4,2,3,1,0:T(8,128)S(1)}, u32[]{:S(2)}, u32[]{:S(2)}) async-start(f32[32,1,8,1,384]{4,2,3,1,0:T(8,128)} %get-tuple-element.103), calls=%async_computation.2 | async-start | bytes 786432 | tf_op jit(solution)/shard_map/all_to_all | solution.py:189
  530.5 7.8 exponential_select_fusion.1
  539.5 9.3 %all-to-all-start.5 = ((f32[32,1,8,1,384]{4,2,3,1,0:T(8,128)}), f32[32,1,8,1,384]{4,2,3,1,0:T(8,128)}, u32[]{:S(2)}, u32[]{:S(2)}) async-start(f32[32,1,8,1,384]{4,2,3,1,0:T(8,128)} %get-tuple-element.101), calls=%async_computation.5 | async-start | bytes 786432 | tf_op jit(solution)/shard_map/all_to_all | solution.py:189
  552.9 7.7 multiply_reduce_fusion.3
  561.9 9.2 %all-to-all-start.11 = ((f32[32,1,8,1,384]{4,2,3,1,0:T(8,128)}), f32[32,1,8,1,384]{4,2,3,1,0:T(8,128)S(1)}, u32[]{:S(2)}, u32[]{:S(2)}) async-start(f32[32,1,8,1,384]{4,2,3,1,0:T(8,128)} %get-tuple-element.102), calls=%async_computation.11 | async-start | bytes 786432 | tf_op jit(solution)/shard_map/all_to_all | solution.py:189
  577.7 7.7 multiply_reduce_fusion.2
  590.9 9.3 %all-to-all-start.8 = ((f32[32,1,8,1,384]{4,2,3,1,0:T(8,128)}), f32[32,1,8,1,384]{4,2,3,1,0:T(8,128)}, u32[]{:S(2)}, u32[]{:S(2)}) async-start(f32[32,1,8,1,384]{4,2,3,1,0:T(8,128)} %get-tuple-element.100), calls=%async_computation.8 | async-start | bytes 786432 | tf_op jit(solution)/shard_map/all_to_all | solution.py:189
  604.5 7.7 multiply_reduce_fusion
  620.3 7.7 multiply_reduce_fusion.1
  631.2 88.7 %all-reduce.7.cloned.1.call-done = (f32[128,1536]{1,0:T(8,128)}, f32[128,1536]{1,0:T(8,128)}, f32[128,1536]{1,0:T(8,128)}, f32[128,1536]{1,0:T(8,128)}) async-done(((f32[128,1536]{1,0:T(8,128)}, f32[128,1536]{1,0:T(8,128)}, f32[128,1536]{1,0:T(8,128)}, f32[128,1536]{1,0:T(8,128)}), (f32[128,1536]{1,0:T(8,128)}, f32[128,1536]{1,0:T(8,128)}, f32[128,1536]{1,0:T(8,128)}, ...) | async-done | bytes 3145744 | tf_op jit(solution)/shard_map/psum | solution.py:238
  719.9 3.0 multiply_reduce_fusion.10
  728.4 4.1 fusion.33
  732.5 4.1 fusion.34
  736.5 3.4 fusion.169
  739.9 4.1 fusion.35
  744.1 3.3 fusion.167
  747.3 4.0 fusion.36
  751.3 76.1 %all-reduce.5.cloned.1.call-done = (f32[128,1536]{1,0:T(8,128)}, f32[128,1536]{1,0:T(8,128)}, f32[128,1536]{1,0:T(8,128)}, f32[128,1536]{1,0:T(8,128)}) async-done(((f32[128,1536]{1,0:T(8,128)}, f32[128,1536]{1,0:T(8,128)}, f32[128,1536]{1,0:T(8,128)}, f32[128,1536]{1,0:T(8,128)}), (f32[128,1536]{1,0:T(8,128)}, f32[128,1536]{1,0:T(8,128)}, f32[128,1536]{1,0:T(8,128)}, ...) | async-done | bytes 3145744 | tf_op jit(solution)/shard_map/psum | solution.py:244
  827.4 4.1 fusion.58
  (463 shorter events, 302.6 us)
Async XLA Ops:
  6.5 721.9 %copy-start = (bf16[1024,1536]{1,0:T(8,128)(2,1)S(1)}, bf16[1024,1536]{1,0:T(8,128)(2,1)}, u32[]{:S(2)}) copy-start(bf16[1024,1536]{1,0:T(8,128)(2,1)} %param.35) | copy-start | bytes 9437188
  6.5 165.9 %all-gather.9.cloned.1.call-start = ((), (), s32[]{:S(2)}) async-start(), calls=%async_computation.15 | async-start | bytes 3244032 | tf_op jit(solution)/shard_map/all_gather | solution.py:135
  15.1 160.7 %all-gather.7.cloned.1.call-start = ((), (), s32[]{:S(2)}) async-start(), calls=%async_computation.14 | async-start | bytes 3244032 | tf_op jit(solution)/shard_map/all_gather | solution.py:135
  15.8 231.1 %all-gather.11.cloned.1.call-start = ((), (), s32[]{:S(2)}) async-start(), calls=%async_computation.16 | async-start | bytes 3244032 | tf_op jit(solution)/shard_map/all_gather | solution.py:135
  17.6 17.3 %copy-start.87 = (pred[16]{0:T(512)(128)(4,1)}, pred[16]{0:T(512)(128)(4,1)S(1)}, u32[]{:S(2)}) copy-start(pred[16]{0:T(512)(128)(4,1)S(1)} %broadcast_compare_fusion) | copy-start | bytes 52
  19.0 150.7 %all-to-all-start = ((f32[32,1,1]{2,1,0:T(1,128)}), f32[32,1,1]{2,1,0:T(1,128)}, u32[]{:S(2)}, u32[]{:S(2)}) async-start(f32[32,1,1]{2,1,0:T(1,128)} %copy.715), calls=%async_computation | async-start | bytes 32768 | tf_op jit(solution)/shard_map/all_to_all | solution.py:152
  30.4 293.4 %all-gather.5.cloned.1.call-start = ((), (), s32[]{:S(2)}) async-start(), calls=%async_computation.13 | async-start | bytes 3244032 | tf_op jit(solution)/shard_map/all_gather | solution.py:135
  87.7 21.9 %copy-start.39 = (f32[32,8,1,6]{1,2,3,0:T(1,128)S(1)}, f32[32,8,1,6]{1,2,3,0:T(1,128)}, u32[]{:S(2)}) copy-start(f32[32,8,1,6]{1,2,3,0:T(1,128)} %get-tuple-element.76) | copy-start | bytes 18436
  105.5 19.6 %copy-start.69 = (f32[128,6]{0,1:T(8,128)S(1)}, f32[128,6]{0,1:T(8,128)}, u32[]{:S(2)}) copy-start(f32[128,6]{0,1:T(8,128)} %copy.815) | copy-start | bytes 9220
  106.5 20.0 %copy-start.53 = (f32[128,6]{0,1:T(8,128)S(1)}, f32[128,6]{0,1:T(8,128)}, u32[]{:S(2)}) copy-start(f32[128,6]{0,1:T(8,128)} %slice_add_fusion.1) | copy-start | bytes 9220
  140.6 14.2 %copy-start.33 = (bf16[2,128,384]{1,2,0:T(8,128)(2,1)S(1)}, bf16[2,128,384]{1,2,0:T(8,128)(2,1)}, u32[]{:S(2)}) copy-start(bf16[2,128,384]{1,2,0:T(8,128)(2,1)} %copy.782) | copy-start | bytes 589828
  148.1 18.0 %copy-start.79 = (s32[16]{0:T(128)S(1)}, s32[16]{0:T(128)}, u32[]{:S(2)}) copy-start(s32[16]{0:T(128)} %copy-done.78) | copy-start | bytes 196
  166.1 226.7 %copy-start.56 = (s32[1024]{0:T(1024)}, s32[1024]{0:T(1024)S(1)}, u32[]{:S(2)}) copy-start(s32[1024]{0:T(1024)S(1)} %pad_clamp_fusion.3) | copy-start | bytes 12292
  264.4 10.9 %copy-start.30 = (f32[16,8,6]{1,2,0:T(8,128)S(1)}, f32[16,8,6]{1,2,0:T(8,128)}, u32[]{:S(2)}) copy-start(f32[16,8,6]{1,2,0:T(8,128)} %get-tuple-element.119) | copy-start | bytes 9220
  327.2 41.9 %copy-start.81 = (pred[32]{0:T(512)(128)(4,1)S(1)}, pred[32]{0:T(512)(128)(4,1)}, u32[]{:S(2)}) copy-start(pred[32]{0:T(512)(128)(4,1)} %fusion.115) | copy-start | bytes 100
  372.1 28.2 %all-to-all-start.1 = ((f32[32,1,8,1,6]{2,3,4,1,0:T(1,128)}), f32[32,1,8,1,6]{2,3,4,1,0:T(1,128)}, u32[]{:S(2)}, u32[]{:S(2)}) async-start(f32[32,1,8,1,6]{2,3,4,1,0:T(1,128)} %copy.724), calls=%async_computation.1 | async-start | bytes 196608 | tf_op jit(solution)/shard_map/all_to_all | solution.py:163
  388.3 21.1 %copy-start.82 = (pred[32]{0:T(512)(128)(4,1)S(1)}, pred[32]{0:T(512)(128)(4,1)}, u32[]{:S(2)}) copy-start(pred[32]{0:T(512)(128)(4,1)} %fusion.115) | copy-start | bytes 100
  394.1 19.5 %copy-start.49 = (f32[32,1,8,1,6]{0,2,4,3,1:T(8,128)S(1)}, f32[32,1,8,1,6]{0,2,4,3,1:T(8,128)}, u32[]{:S(2)}) copy-start(f32[32,1,8,1,6]{0,2,4,3,1:T(8,128)} %get-tuple-element.110) | copy-start | bytes 18436
  394.1 20.3 %copy-start.48 = (f32[32,1,8,1,6]{0,2,4,3,1:T(8,128)S(1)}, f32[32,1,8,1,6]{0,2,4,3,1:T(8,128)}, u32[]{:S(2)}) copy-start(f32[32,1,8,1,6]{0,2,4,3,1:T(8,128)} %get-tuple-element.107) | copy-start | bytes 18436
  394.1 21.0 %copy-start.47 = (f32[32,1,8,1,6]{0,2,4,3,1:T(8,128)S(1)}, f32[32,1,8,1,6]{0,2,4,3,1:T(8,128)}, u32[]{:S(2)}) copy-start(f32[32,1,8,1,6]{0,2,4,3,1:T(8,128)} %get-tuple-element.109) | copy-start | bytes 18436
  394.1 21.7 %copy-start.46 = (f32[32,1,8,1,6]{0,2,4,3,1:T(8,128)S(1)}, f32[32,1,8,1,6]{0,2,4,3,1:T(8,128)}, u32[]{:S(2)}) copy-start(f32[32,1,8,1,6]{0,2,4,3,1:T(8,128)} %get-tuple-element.104) | copy-start | bytes 18436
  396.0 30.8 %copy-start.44 = (f32[32,8,1,6]{0,1,3,2:T(8,128)S(1)}, f32[32,8,1,6]{0,1,3,2:T(8,128)}, u32[]{:S(2)}) copy-start(f32[32,8,1,6]{0,1,3,2:T(8,128)} %copy.726) | copy-start | bytes 18436
  396.0 30.8 %copy-start.45 = (f32[32,8,1,6]{0,1,3,2:T(8,128)S(1)}, f32[32,8,1,6]{0,1,3,2:T(8,128)}, u32[]{:S(2)}) copy-start(f32[32,8,1,6]{0,1,3,2:T(8,128)} %copy.747) | copy-start | bytes 18436
  397.2 55.7 %copy-start.42 = (f32[32,8,1,6]{0,1,3,2:T(8,128)S(1)}, f32[32,8,1,6]{0,1,3,2:T(8,128)}, u32[]{:S(2)}) copy-start(f32[32,8,1,6]{0,1,3,2:T(8,128)} %copy.773) | copy-start | bytes 18436
  397.2 55.7 %copy-start.43 = (f32[32,8,1,6]{0,1,3,2:T(8,128)S(1)}, f32[32,8,1,6]{0,1,3,2:T(8,128)}, u32[]{:S(2)}) copy-start(f32[32,8,1,6]{0,1,3,2:T(8,128)} %copy.805) | copy-start | bytes 18436
  398.8 13.4 %copy-start.51 = (f32[32,1,8,1,6]{0,2,4,3,1:T(8,128)S(1)}, f32[32,1,8,1,6]{0,2,4,3,1:T(8,128)}, u32[]{:S(2)}) copy-start(f32[32,1,8,1,6]{0,2,4,3,1:T(8,128)} %get-tuple-element.105) | copy-start | bytes 18436
  398.8 14.1 %copy-start.50 = (f32[32,1,8,1,6]{0,2,4,3,1:T(8,128)S(1)}, f32[32,1,8,1,6]{0,2,4,3,1:T(8,128)}, u32[]{:S(2)}) copy-start(f32[32,1,8,1,6]{0,2,4,3,1:T(8,128)} %get-tuple-element.108) | copy-start | bytes 18436
  400.3 18.1 %all-to-all-start.4 = ((f32[32,1,8,1,6]{2,3,4,1,0:T(1,128)}), f32[32,1,8,1,6]{2,3,4,1,0:T(1,128)S(1)}, u32[]{:S(2)}, u32[]{:S(2)}) async-start(f32[32,1,8,1,6]{2,3,4,1,0:T(1,128)} %copy.745), calls=%async_computation.4 | async-start | bytes 196608 | tf_op jit(solution)/shard_map/all_to_all | solution.py:163
  418.4 17.3 %all-to-all-start.7 = ((f32[32,1,8,1,6]{2,3,4,1,0:T(1,128)}), f32[32,1,8,1,6]{2,3,4,1,0:T(1,128)S(1)}, u32[]{:S(2)}, u32[]{:S(2)}) async-start(f32[32,1,8,1,6]{2,3,4,1,0:T(1,128)} %copy.771), calls=%async_computation.7 | async-start | bytes 196608 | tf_op jit(solution)/shard_map/all_to_all | solution.py:163
  426.9 76.8 %copy-start.34 = (f32[64,8,6]{0,1,2:T(8,128)}, f32[64,8,6]{0,1,2:T(8,128)S(1)}, u32[]{:S(2)}) copy-start(f32[64,8,6]{0,1,2:T(8,128)S(1)} %get-tuple-element.124) | copy-start | bytes 36868
  435.6 12.7 %all-to-all-start.10 = ((f32[32,1,8,1,6]{2,3,4,1,0:T(1,128)}), f32[32,1,8,1,6]{2,3,4,1,0:T(1,128)S(1)}, u32[]{:S(2)}, u32[]{:S(2)}) async-start(f32[32,1,8,1,6]{2,3,4,1,0:T(1,128)} %copy.803), calls=%async_computation.10 | async-start | bytes 196608 | tf_op jit(solution)/shard_map/all_to_all | solution.py:163
  440.8 62.9 %copy-start.27 = (f32[16,8,6]{1,2,0:T(8,128)}, f32[16,8,6]{1,2,0:T(8,128)S(1)}, u32[]{:S(2)}) copy-start(f32[16,8,6]{1,2,0:T(8,128)S(1)} %select_reduce_fusion.3) | copy-start | bytes 9220
  448.4 12.7 %all-to-all-start.3 = ((f32[32,1,8,1,6]{2,3,4,1,0:T(1,128)}), f32[32,1,8,1,6]{2,3,4,1,0:T(1,128)S(1)}, u32[]{:S(2)}, u32[]{:S(2)}) async-start(f32[32,1,8,1,6]{2,3,4,1,0:T(1,128)} %copy.737), calls=%async_computation.3 | async-start | bytes 196608 | tf_op jit(solution)/shard_map/all_to_all | solution.py:176
  453.7 50.0 %copy-start.35 = (f32[64,8,6]{0,1,2:T(8,128)}, f32[64,8,6]{0,1,2:T(8,128)S(1)}, u32[]{:S(2)}) copy-start(f32[64,8,6]{0,1,2:T(8,128)S(1)} %get-tuple-element.125) | copy-start | bytes 36868
  453.8 50.0 %copy-start.36 = (f32[64,8,6]{0,1,2:T(8,128)}, f32[64,8,6]{0,1,2:T(8,128)S(1)}, u32[]{:S(2)}) copy-start(f32[64,8,6]{0,1,2:T(8,128)S(1)} %get-tuple-element.126) | copy-start | bytes 36868
  461.1 12.8 %all-to-all-start.12 = ((f32[32,1,8,1,6]{2,3,4,1,0:T(1,128)}), f32[32,1,8,1,6]{2,3,4,1,0:T(1,128)S(1)}, u32[]{:S(2)}, u32[]{:S(2)}) async-start(f32[32,1,8,1,6]{2,3,4,1,0:T(1,128)} %copy.826), calls=%async_computation.12 | async-start | bytes 196608 | tf_op jit(solution)/shard_map/all_to_all | solution.py:176
  473.9 13.4 %all-to-all-start.6 = ((f32[32,1,8,1,6]{2,3,4,1,0:T(1,128)}), f32[32,1,8,1,6]{2,3,4,1,0:T(1,128)}, u32[]{:S(2)}, u32[]{:S(2)}) async-start(f32[32,1,8,1,6]{2,3,4,1,0:T(1,128)} %copy.763), calls=%async_computation.6 | async-start | bytes 196608 | tf_op jit(solution)/shard_map/all_to_all | solution.py:176
  480.4 23.4 %copy-start.24 = (f32[16,8,6]{1,2,0:T(8,128)}, f32[16,8,6]{1,2,0:T(8,128)S(1)}, u32[]{:S(2)}) copy-start(f32[16,8,6]{1,2,0:T(8,128)S(1)} %get-tuple-element.10) | copy-start | bytes 9220
  480.4 23.4 %copy-start.25 = (f32[16,8,6]{1,2,0:T(8,128)}, f32[16,8,6]{1,2,0:T(8,128)S(1)}, u32[]{:S(2)}) copy-start(f32[16,8,6]{1,2,0:T(8,128)S(1)} %get-tuple-element.11) | copy-start | bytes 9220
  480.4 23.4 %copy-start.26 = (f32[16,8,6]{1,2,0:T(8,128)}, f32[16,8,6]{1,2,0:T(8,128)S(1)}, u32[]{:S(2)}) copy-start(f32[16,8,6]{1,2,0:T(8,128)S(1)} %get-tuple-element.12) | copy-start | bytes 9220
  487.3 16.4 %all-to-all-start.9 = ((f32[32,1,8,1,6]{2,3,4,1,0:T(1,128)}), f32[32,1,8,1,6]{2,3,4,1,0:T(1,128)}, u32[]{:S(2)}, u32[]{:S(2)}) async-start(f32[32,1,8,1,6]{2,3,4,1,0:T(1,128)} %copy.794), calls=%async_computation.9 | async-start | bytes 196608 | tf_op jit(solution)/shard_map/all_to_all | solution.py:176
  503.8 35.7 %all-to-all-start.2 = ((f32[32,1,8,1,384]{4,2,3,1,0:T(8,128)}), f32[32,1,8,1,384]{4,2,3,1,0:T(8,128)S(1)}, u32[]{:S(2)}, u32[]{:S(2)}) async-start(f32[32,1,8,1,384]{4,2,3,1,0:T(8,128)} %get-tuple-element.103), calls=%async_computation.2 | async-start | bytes 786432 | tf_op jit(solution)/shard_map/all_to_all | solution.py:189
  539.5 22.4 %all-to-all-start.5 = ((f32[32,1,8,1,384]{4,2,3,1,0:T(8,128)}), f32[32,1,8,1,384]{4,2,3,1,0:T(8,128)}, u32[]{:S(2)}, u32[]{:S(2)}) async-start(f32[32,1,8,1,384]{4,2,3,1,0:T(8,128)} %get-tuple-element.101), calls=%async_computation.5 | async-start | bytes 786432 | tf_op jit(solution)/shard_map/all_to_all | solution.py:189
  561.9 28.9 %all-to-all-start.11 = ((f32[32,1,8,1,384]{4,2,3,1,0:T(8,128)}), f32[32,1,8,1,384]{4,2,3,1,0:T(8,128)S(1)}, u32[]{:S(2)}, u32[]{:S(2)}) async-start(f32[32,1,8,1,384]{4,2,3,1,0:T(8,128)} %get-tuple-element.102), calls=%async_computation.11 | async-start | bytes 786432 | tf_op jit(solution)/shard_map/all_to_all | solution.py:189
  590.9 24.4 %all-to-all-start.8 = ((f32[32,1,8,1,384]{4,2,3,1,0:T(8,128)}), f32[32,1,8,1,384]{4,2,3,1,0:T(8,128)}, u32[]{:S(2)}, u32[]{:S(2)}) async-start(f32[32,1,8,1,384]{4,2,3,1,0:T(8,128)} %get-tuple-element.100), calls=%async_computation.8 | async-start | bytes 786432 | tf_op jit(solution)/shard_map/all_to_all | solution.py:189
  600.2 119.6 %all-reduce.7.cloned.1.call-start = ((), (), s32[]{:S(2)}) async-start(), calls=%async_computation.18 | async-start | bytes 6291456 | tf_op jit(solution)/shard_map/psum | solution.py:238
  631.1 91.7 %copy-start.76 = (f32[1536]{0:T(1024)S(1)}, f32[1536]{0:T(1024)}, u32[]{:S(2)}) copy-start(f32[1536]{0:T(1024)} %param.32) | copy-start | bytes 18436
  631.1 196.3 %all-reduce.5.cloned.1.call-start = ((), (), s32[]{:S(2)}) async-start(), calls=%async_computation.17 | async-start | bytes 6291456 | tf_op jit(solution)/shard_map/psum | solution.py:244
  (63 other events, 326.7 us)
Sparse Core Ops, SparseCore 0:
  15.2 77.4 all-gather.8
  95.7 74.0 all-gather.6
  172.8 74.0 all-gather.10
  249.7 74.0 all-gather.4
  631.3 88.5 all-reduce.6
  751.5 75.9 all-reduce.4
where the time goes:
time: 854 us; the launch traced here: 840 us
  waiting for transfers between devices  319 us (37%)
  local copies, waits for them, and re-layouts  223 us (26%)
  other arithmetic  123 us (14%)
  starting transfers between devices  93.1 us (11%)
  matrix products  66.5 us (8%)
  between operations  14.9 us (2%)
    all_gather x4, waiting for transfers between devices, shards(): gathered = lax.all_gather(query_block, 'group', axis=0, tiled=True)  115 us
    psum x1, waiting for transfers between devices, shards(): lax.psum(jnp.dot(attended, w_out, preferred_element_type=jnp.float32), 'h...  88.7 us
    psum x1, waiting for transfers between devices, shards(): lax.psum(jnp.dot(hidden, w_down, preferred_element_type=jnp.float32), 'he...  76.1 us
    all_to_all x4, starting transfers between devices, shards(): lax.all_to_all(jnp.where(full_slot, numerator[slot_source], 0.0), 'group'...  37 us
    reduce_sum x4, other arithmetic, by_request(): combined = jnp.sum(factor[..., None] * numer_split[None], axis=1)  30.9 us
    all_to_all x4, starting transfers between devices, shards(): lax.all_to_all(jnp.where(full_slot, page_top[slot_source], masked_score),...  27.4 us
    all_to_all x4, waiting for transfers between devices, shards(): lax.all_to_all(jnp.where(full_slot, page_total[slot_source], 0.0), 'group...  21.2 us
  transfers between devices with their start and end apart: 19, of which 11 were waited for; matrix products, arithmetic and copies ran while one was open for 36% of the time, Pallas kernels for 0%

commit v1 on v0

--- a/solution.py
+++ b/solution.py
@@ -241,7 +241,9 @@
         gate_proj = jnp.dot(normed_ffn, w_gate, preferred_element_type=jnp.float32)
         up_proj = jnp.dot(normed_ffn, w_up, preferred_element_type=jnp.float32)
         hidden = (jax.nn.silu(gate_proj) * up_proj).astype(jnp.bfloat16)
-        down_sum = lax.psum(jnp.dot(hidden, w_down, preferred_element_type=jnp.float32), "head")
+        own = jnp.dot(hidden, w_down, preferred_element_type=jnp.float32)
+        blocks = lax.all_gather(own, "head", axis=0, tiled=False)
+        down_sum = blocks.sum(axis=0)
         finished.append((residual + down_sum).astype(jnp.bfloat16))
     result = jnp.stack(finished, axis=0)
     return result

time: 854 us -> 921 us (1.078)
  waiting for transfers between devices: 319 us -> 371 us
  other arithmetic: 123 us -> 136 us
    all_gather x0 -> x4, waiting for transfers between devices: none -> 128 us  [shards(): blocks = lax.all_gather(own, 'head', axis=0, tiled=False)]
    psum x1 -> x0, waiting for transfers between devices: 76.1 us -> none  [shards(): lax.psum(jnp.dot(hidden, w_down, preferred_element_type=jnp.float32), 'he...]
    reduce_sum x0 -> x4, other arithmetic: none -> 12.4 us  [shards(): down_sum = blocks.sum(axis=0)]
  transfers between devices with their start and end apart: 19 -> 22, of which waited for: 11 -> 14; matrix products, arithmetic and copies ran while one was open for 36% -> 37% of each run, Pallas kernels for 0% -> 0%
where the time goes in v1:
time: 921 us; the launch traced here: 907 us
  waiting for transfers between devices  371 us (40%)
  local copies, waits for them, and re-layouts  224 us (24%)
  other arithmetic  136 us (15%)
  starting transfers between devices  93.3 us (10%)
  matrix products  68.9 us (7%)
  between operations  14.9 us (2%)
    all_gather x4, waiting for transfers between devices, shards(): blocks = lax.all_gather(own, 'head', axis=0, tiled=False)  128 us
    all_gather x4, waiting for transfers between devices, shards(): gathered = lax.all_gather(query_block, 'group', axis=0, tiled=True)  114 us
    psum x1, waiting for transfers between devices, shards(): lax.psum(jnp.dot(attended, w_out, preferred_element_type=jnp.float32), 'h...  88.7 us
    all_to_all x4, starting transfers between devices, shards(): lax.all_to_all(jnp.where(full_slot, numerator[slot_source], 0.0), 'group'...  37 us
    reduce_sum x4, other arithmetic, by_request(): combined = jnp.sum(factor[..., None] * numer_split[None], axis=1)  30.9 us
    all_to_all x4, starting transfers between devices, shards(): lax.all_to_all(jnp.where(full_slot, page_top[slot_source], masked_score),...  27.1 us
    all_to_all x4, waiting for transfers between devices, shards(): lax.all_to_all(jnp.where(full_slot, page_total[slot_source], 0.0), 'group...  21.2 us
  transfers between devices with their start and end apart: 22, of which 14 were waited for; matrix products, arithmetic and copies ran while one was open for 37% of the time, Pallas kernels for 0%

profile of v1, /device:TPU:1, one launch (start us, length us, event | category | flops | bytes accessed | tf_op | source)
XLA Modules:
  0.0 907.2 jit_solution(17637661946772282779)
XLA Ops:
  19.1 11.5 %all-to-all-start = ((f32[32,1,1]{2,1,0:T(1,128)}), f32[32,1,1]{2,1,0:T(1,128)}, u32[]{:S(2)}, u32[]{:S(2)}) async-start(f32[32,1,1]{2,1,0:T(1,128)} %copy.715), calls=%async_computation | async-start | bytes 32768 | tf_op jit(solution)/shard_map/all_to_all | solution.py:152
  36.0 3.9 slice.193
  43.7 3.7 reshape.1148
  47.4 3.8 bitcast_reduce_fusion
  56.7 4.7 copy.728
  61.4 4.6 reshape.1155
  179.7 67.2 %all-gather.19.cloned.1.call-done = bf16[4096,1,384]{2,0,1:T(8,128)(2,1)} async-done(((bf16[128,1,384]{2,0,1:T(8,128)(2,1)}), bf16[4096,1,384]{2,0,1:T(8,128)(2,1)}) %all-gather.19.cloned.1.call-update) | async-done | bytes 3145744 | tf_op jit(solution)/shard_map/all_gather | solution.py:135
  254.5 3.3 fusion.162
  259.5 3.4 fusion.164
  270.3 3.3 convolution_bitcast_fusion.2
  277.1 46.7 %all-gather.13.cloned.1.call-done = bf16[4096,1,384]{2,0,1:T(8,128)(2,1)} async-done(((bf16[128,1,384]{2,0,1:T(8,128)(2,1)}), bf16[4096,1,384]{2,0,1:T(8,128)(2,1)}) %all-gather.13.cloned.1.call-update) | async-done | bytes 3145744 | tf_op jit(solution)/shard_map/all_gather | solution.py:135
  372.2 5.6 all-to-all-start.1
  377.8 3.2 convolution_bitcast_fusion.4
  400.4 9.2 %all-to-all-start.4 = ((f32[32,1,8,1,6]{2,3,4,1,0:T(1,128)}), f32[32,1,8,1,6]{2,3,4,1,0:T(1,128)S(1)}, u32[]{:S(2)}, u32[]{:S(2)}) async-start(f32[32,1,8,1,6]{2,3,4,1,0:T(1,128)} %copy.745), calls=%async_computation.4 | async-start | bytes 196608 | tf_op jit(solution)/shard_map/all_to_all | solution.py:163
  418.5 8.4 all-to-all-start.7
  427.1 8.7 all-to-all-done.7
  435.8 4.0 all-to-all-start.10
  441.3 7.2 all-to-all-done.10
  448.5 3.8 all-to-all-start.3
  454.0 7.3 all-to-all-done.3
  461.3 3.9 all-to-all-start.12
  466.1 8.0 all-to-all-done.12
  474.0 4.6 all-to-all-start.6
  481.6 5.9 all-to-all-done.6
  487.5 4.6 all-to-all-start.9
  504.0 9.2 %all-to-all-start.2 = ((f32[32,1,8,1,384]{4,2,3,1,0:T(8,128)}), f32[32,1,8,1,384]{4,2,3,1,0:T(8,128)S(1)}, u32[]{:S(2)}, u32[]{:S(2)}) async-start(f32[32,1,8,1,384]{4,2,3,1,0:T(8,128)} %get-tuple-element.99), calls=%async_computation.2 | async-start | bytes 786432 | tf_op jit(solution)/shard_map/all_to_all | solution.py:189
  530.7 7.8 exponential_select_fusion.1
  539.8 9.3 %all-to-all-start.5 = ((f32[32,1,8,1,384]{4,2,3,1,0:T(8,128)}), f32[32,1,8,1,384]{4,2,3,1,0:T(8,128)}, u32[]{:S(2)}, u32[]{:S(2)}) async-start(f32[32,1,8,1,384]{4,2,3,1,0:T(8,128)} %get-tuple-element.97), calls=%async_computation.5 | async-start | bytes 786432 | tf_op jit(solution)/shard_map/all_to_all | solution.py:189
  553.2 7.7 multiply_reduce_fusion.3
  562.2 9.2 %all-to-all-start.11 = ((f32[32,1,8,1,384]{4,2,3,1,0:T(8,128)}), f32[32,1,8,1,384]{4,2,3,1,0:T(8,128)S(1)}, u32[]{:S(2)}, u32[]{:S(2)}) async-start(f32[32,1,8,1,384]{4,2,3,1,0:T(8,128)} %get-tuple-element.98), calls=%async_computation.11 | async-start | bytes 786432 | tf_op jit(solution)/shard_map/all_to_all | solution.py:189
  578.0 7.7 multiply_reduce_fusion.2
  591.1 9.3 %all-to-all-start.8 = ((f32[32,1,8,1,384]{4,2,3,1,0:T(8,128)}), f32[32,1,8,1,384]{4,2,3,1,0:T(8,128)}, u32[]{:S(2)}, u32[]{:S(2)}) async-start(f32[32,1,8,1,384]{4,2,3,1,0:T(8,128)} %get-tuple-element.96), calls=%async_computation.8 | async-start | bytes 786432 | tf_op jit(solution)/shard_map/all_to_all | solution.py:189
  604.7 7.7 multiply_reduce_fusion
  620.6 7.7 multiply_reduce_fusion.1
  631.5 88.7 %all-reduce.3.cloned.1.call-done = (f32[128,1536]{1,0:T(8,128)}, f32[128,1536]{1,0:T(8,128)}, f32[128,1536]{1,0:T(8,128)}, f32[128,1536]{1,0:T(8,128)}) async-done(((f32[128,1536]{1,0:T(8,128)}, f32[128,1536]{1,0:T(8,128)}, f32[128,1536]{1,0:T(8,128)}, f32[128,1536]{1,0:T(8,128)}), (f32[128,1536]{1,0:T(8,128)}, f32[128,1536]{1,0:T(8,128)}, f32[128,1536]{1,0:T(8,128)}, ...) | async-done | bytes 3145744 | tf_op jit(solution)/shard_map/psum | solution.py:238
  727.5 4.1 fusion.36
  731.6 3.4 fusion.171
  735.0 4.1 fusion.34
  739.2 3.4 fusion.169
  742.6 4.3 fusion.35
  747.3 3.2 fusion.173
  750.5 4.0 fusion.33
  754.6 16.0 %all-gather.21.cloned.1.call-done = f32[512,1536]{1,0:T(8,128)} async-done(((f32[128,1536]{1,0:T(8,128)}), f32[512,1536]{1,0:T(8,128)}) %all-gather.21.cloned.1.call-update) | async-done | bytes 3145744 | tf_op jit(solution)/shard_map/all_gather | solution.py:245
  773.6 37.3 %all-gather.25.cloned.1.call-done = f32[512,1536]{1,0:T(8,128)} async-done(((f32[128,1536]{1,0:T(8,128)}), f32[512,1536]{1,0:T(8,128)}) %all-gather.25.cloned.1.call-update) | async-done | bytes 3145744 | tf_op jit(solution)/shard_map/all_gather | solution.py:245
  814.0 37.3 %all-gather.23.cloned.1.call-done = f32[512,1536]{1,0:T(8,128)} async-done(((f32[128,1536]{1,0:T(8,128)}), f32[512,1536]{1,0:T(8,128)}) %all-gather.23.cloned.1.call-update) | async-done | bytes 3145744 | tf_op jit(solution)/shard_map/all_gather | solution.py:245
  851.3 3.1 reduce_sum.284
  854.4 37.3 %all-gather.27.cloned.1.call-done = f32[512,1536]{1,0:T(8,128)} async-done(((f32[128,1536]{1,0:T(8,128)}), f32[512,1536]{1,0:T(8,128)}) %all-gather.27.cloned.1.call-update) | async-done | bytes 3145744 | tf_op jit(solution)/shard_map/all_gather | solution.py:245
  894.8 4.1 fusion.58
  (474 shorter events, 325.8 us)
Async XLA Ops:
  6.5 720.9 %copy-start = (bf16[1024,1536]{1,0:T(8,128)(2,1)S(1)}, bf16[1024,1536]{1,0:T(8,128)(2,1)}, u32[]{:S(2)}) copy-start(bf16[1024,1536]{1,0:T(8,128)(2,1)} %param.35) | copy-start | bytes 9437188
  6.5 166.4 %all-gather.17.cloned.1.call-start = ((), (), s32[]{:S(2)}) async-start(), calls=%async_computation.15 | async-start | bytes 3244032 | tf_op jit(solution)/shard_map/all_gather | solution.py:135
  15.1 161.3 %all-gather.15.cloned.1.call-start = ((), (), s32[]{:S(2)}) async-start(), calls=%async_computation.14 | async-start | bytes 3244032 | tf_op jit(solution)/shard_map/all_gather | solution.py:135
  15.8 231.1 %all-gather.19.cloned.1.call-start = ((), (), s32[]{:S(2)}) async-start(), calls=%async_computation.16 | async-start | bytes 3244032 | tf_op jit(solution)/shard_map/all_gather | solution.py:135
  17.8 17.4 %copy-start.86 = (pred[16]{0:T(512)(128)(4,1)}, pred[16]{0:T(512)(128)(4,1)S(1)}, u32[]{:S(2)}) copy-start(pred[16]{0:T(512)(128)(4,1)S(1)} %broadcast_compare_fusion) | copy-start | bytes 52
  19.1 151.2 %all-to-all-start = ((f32[32,1,1]{2,1,0:T(1,128)}), f32[32,1,1]{2,1,0:T(1,128)}, u32[]{:S(2)}, u32[]{:S(2)}) async-start(f32[32,1,1]{2,1,0:T(1,128)} %copy.715), calls=%async_computation | async-start | bytes 32768 | tf_op jit(solution)/shard_map/all_to_all | solution.py:152
  30.6 293.3 %all-gather.13.cloned.1.call-start = ((), (), s32[]{:S(2)}) async-start(), calls=%async_computation.13 | async-start | bytes 3244032 | tf_op jit(solution)/shard_map/all_gather | solution.py:135
  87.9 22.0 %copy-start.38 = (f32[32,8,1,6]{1,2,3,0:T(1,128)S(1)}, f32[32,8,1,6]{1,2,3,0:T(1,128)}, u32[]{:S(2)}) copy-start(f32[32,8,1,6]{1,2,3,0:T(1,128)} %get-tuple-element.72) | copy-start | bytes 18436
  105.8 19.7 %copy-start.68 = (f32[128,6]{0,1:T(8,128)S(1)}, f32[128,6]{0,1:T(8,128)}, u32[]{:S(2)}) copy-start(f32[128,6]{0,1:T(8,128)} %copy.815) | copy-start | bytes 9220
  106.7 20.0 %copy-start.52 = (f32[128,6]{0,1:T(8,128)S(1)}, f32[128,6]{0,1:T(8,128)}, u32[]{:S(2)}) copy-start(f32[128,6]{0,1:T(8,128)} %slice_add_fusion.1) | copy-start | bytes 9220
  141.0 14.3 %copy-start.32 = (bf16[2,128,384]{1,2,0:T(8,128)(2,1)S(1)}, bf16[2,128,384]{1,2,0:T(8,128)(2,1)}, u32[]{:S(2)}) copy-start(bf16[2,128,384]{1,2,0:T(8,128)(2,1)} %copy.782) | copy-start | bytes 589828
  148.4 18.1 %copy-start.78 = (s32[16]{0:T(128)S(1)}, s32[16]{0:T(128)}, u32[]{:S(2)}) copy-start(s32[16]{0:T(128)} %copy-done.77) | copy-start | bytes 196
  166.5 226.3 %copy-start.55 = (s32[1024]{0:T(1024)}, s32[1024]{0:T(1024)S(1)}, u32[]{:S(2)}) copy-start(s32[1024]{0:T(1024)S(1)} %pad_clamp_fusion.3) | copy-start | bytes 12292
  327.2 42.0 %copy-start.80 = (pred[32]{0:T(512)(128)(4,1)S(1)}, pred[32]{0:T(512)(128)(4,1)}, u32[]{:S(2)}) copy-start(pred[32]{0:T(512)(128)(4,1)} %fusion.115) | copy-start | bytes 100
  372.2 28.2 %all-to-all-start.1 = ((f32[32,1,8,1,6]{2,3,4,1,0:T(1,128)}), f32[32,1,8,1,6]{2,3,4,1,0:T(1,128)}, u32[]{:S(2)}, u32[]{:S(2)}) async-start(f32[32,1,8,1,6]{2,3,4,1,0:T(1,128)} %copy.724), calls=%async_computation.1 | async-start | bytes 196608 | tf_op jit(solution)/shard_map/all_to_all | solution.py:163
  388.5 21.1 %copy-start.81 = (pred[32]{0:T(512)(128)(4,1)S(1)}, pred[32]{0:T(512)(128)(4,1)}, u32[]{:S(2)}) copy-start(pred[32]{0:T(512)(128)(4,1)} %fusion.115) | copy-start | bytes 100
  394.2 19.5 %copy-start.48 = (f32[32,1,8,1,6]{0,2,4,3,1:T(8,128)S(1)}, f32[32,1,8,1,6]{0,2,4,3,1:T(8,128)}, u32[]{:S(2)}) copy-start(f32[32,1,8,1,6]{0,2,4,3,1:T(8,128)} %get-tuple-element.106) | copy-start | bytes 18436
  394.2 20.3 %copy-start.47 = (f32[32,1,8,1,6]{0,2,4,3,1:T(8,128)S(1)}, f32[32,1,8,1,6]{0,2,4,3,1:T(8,128)}, u32[]{:S(2)}) copy-start(f32[32,1,8,1,6]{0,2,4,3,1:T(8,128)} %get-tuple-element.103) | copy-start | bytes 18436
  394.2 21.0 %copy-start.46 = (f32[32,1,8,1,6]{0,2,4,3,1:T(8,128)S(1)}, f32[32,1,8,1,6]{0,2,4,3,1:T(8,128)}, u32[]{:S(2)}) copy-start(f32[32,1,8,1,6]{0,2,4,3,1:T(8,128)} %get-tuple-element.105) | copy-start | bytes 18436
  394.2 21.7 %copy-start.45 = (f32[32,1,8,1,6]{0,2,4,3,1:T(8,128)S(1)}, f32[32,1,8,1,6]{0,2,4,3,1:T(8,128)}, u32[]{:S(2)}) copy-start(f32[32,1,8,1,6]{0,2,4,3,1:T(8,128)} %get-tuple-element.100) | copy-start | bytes 18436
  396.2 30.8 %copy-start.43 = (f32[32,8,1,6]{0,1,3,2:T(8,128)S(1)}, f32[32,8,1,6]{0,1,3,2:T(8,128)}, u32[]{:S(2)}) copy-start(f32[32,8,1,6]{0,1,3,2:T(8,128)} %copy.726) | copy-start | bytes 18436
  396.2 30.8 %copy-start.44 = (f32[32,8,1,6]{0,1,3,2:T(8,128)S(1)}, f32[32,8,1,6]{0,1,3,2:T(8,128)}, u32[]{:S(2)}) copy-start(f32[32,8,1,6]{0,1,3,2:T(8,128)} %copy.747) | copy-start | bytes 18436
  397.3 55.7 %copy-start.41 = (f32[32,8,1,6]{0,1,3,2:T(8,128)S(1)}, f32[32,8,1,6]{0,1,3,2:T(8,128)}, u32[]{:S(2)}) copy-start(f32[32,8,1,6]{0,1,3,2:T(8,128)} %copy.773) | copy-start | bytes 18436
  397.3 55.7 %copy-start.42 = (f32[32,8,1,6]{0,1,3,2:T(8,128)S(1)}, f32[32,8,1,6]{0,1,3,2:T(8,128)}, u32[]{:S(2)}) copy-start(f32[32,8,1,6]{0,1,3,2:T(8,128)} %copy.805) | copy-start | bytes 18436
  400.4 18.1 %all-to-all-start.4 = ((f32[32,1,8,1,6]{2,3,4,1,0:T(1,128)}), f32[32,1,8,1,6]{2,3,4,1,0:T(1,128)S(1)}, u32[]{:S(2)}, u32[]{:S(2)}) async-start(f32[32,1,8,1,6]{2,3,4,1,0:T(1,128)} %copy.745), calls=%async_computation.4 | async-start | bytes 196608 | tf_op jit(solution)/shard_map/all_to_all | solution.py:163
  418.5 17.3 %all-to-all-start.7 = ((f32[32,1,8,1,6]{2,3,4,1,0:T(1,128)}), f32[32,1,8,1,6]{2,3,4,1,0:T(1,128)S(1)}, u32[]{:S(2)}, u32[]{:S(2)}) async-start(f32[32,1,8,1,6]{2,3,4,1,0:T(1,128)} %copy.771), calls=%async_computation.7 | async-start | bytes 196608 | tf_op jit(solution)/shard_map/all_to_all | solution.py:163
  427.1 76.9 %copy-start.33 = (f32[64,8,6]{0,1,2:T(8,128)}, f32[64,8,6]{0,1,2:T(8,128)S(1)}, u32[]{:S(2)}) copy-start(f32[64,8,6]{0,1,2:T(8,128)S(1)} %get-tuple-element.120) | copy-start | bytes 36868
  435.8 12.7 %all-to-all-start.10 = ((f32[32,1,8,1,6]{2,3,4,1,0:T(1,128)}), f32[32,1,8,1,6]{2,3,4,1,0:T(1,128)S(1)}, u32[]{:S(2)}, u32[]{:S(2)}) async-start(f32[32,1,8,1,6]{2,3,4,1,0:T(1,128)} %copy.803), calls=%async_computation.10 | async-start | bytes 196608 | tf_op jit(solution)/shard_map/all_to_all | solution.py:163
  440.6 63.4 %copy-start.26 = (f32[16,8,6]{1,2,0:T(8,128)}, f32[16,8,6]{1,2,0:T(8,128)S(1)}, u32[]{:S(2)}) copy-start(f32[16,8,6]{1,2,0:T(8,128)S(1)} %select_reduce_fusion.3) | copy-start | bytes 9220
  448.5 12.8 %all-to-all-start.3 = ((f32[32,1,8,1,6]{2,3,4,1,0:T(1,128)}), f32[32,1,8,1,6]{2,3,4,1,0:T(1,128)S(1)}, u32[]{:S(2)}, u32[]{:S(2)}) async-start(f32[32,1,8,1,6]{2,3,4,1,0:T(1,128)} %copy.737), calls=%async_computation.3 | async-start | bytes 196608 | tf_op jit(solution)/shard_map/all_to_all | solution.py:176
  453.9 50.1 %copy-start.34 = (f32[64,8,6]{0,1,2:T(8,128)}, f32[64,8,6]{0,1,2:T(8,128)S(1)}, u32[]{:S(2)}) copy-start(f32[64,8,6]{0,1,2:T(8,128)S(1)} %get-tuple-element.121) | copy-start | bytes 36868
  453.9 50.1 %copy-start.35 = (f32[64,8,6]{0,1,2:T(8,128)}, f32[64,8,6]{0,1,2:T(8,128)S(1)}, u32[]{:S(2)}) copy-start(f32[64,8,6]{0,1,2:T(8,128)S(1)} %get-tuple-element.122) | copy-start | bytes 36868
  461.3 12.8 %all-to-all-start.12 = ((f32[32,1,8,1,6]{2,3,4,1,0:T(1,128)}), f32[32,1,8,1,6]{2,3,4,1,0:T(1,128)S(1)}, u32[]{:S(2)}, u32[]{:S(2)}) async-start(f32[32,1,8,1,6]{2,3,4,1,0:T(1,128)} %copy.826), calls=%async_computation.12 | async-start | bytes 196608 | tf_op jit(solution)/shard_map/all_to_all | solution.py:176
  474.0 13.5 %all-to-all-start.6 = ((f32[32,1,8,1,6]{2,3,4,1,0:T(1,128)}), f32[32,1,8,1,6]{2,3,4,1,0:T(1,128)}, u32[]{:S(2)}, u32[]{:S(2)}) async-start(f32[32,1,8,1,6]{2,3,4,1,0:T(1,128)} %copy.763), calls=%async_computation.6 | async-start | bytes 196608 | tf_op jit(solution)/shard_map/all_to_all | solution.py:176
  480.5 23.5 %copy-start.23 = (f32[16,8,6]{1,2,0:T(8,128)}, f32[16,8,6]{1,2,0:T(8,128)S(1)}, u32[]{:S(2)}) copy-start(f32[16,8,6]{1,2,0:T(8,128)S(1)} %get-tuple-element.10) | copy-start | bytes 9220
  480.5 23.5 %copy-start.24 = (f32[16,8,6]{1,2,0:T(8,128)}, f32[16,8,6]{1,2,0:T(8,128)S(1)}, u32[]{:S(2)}) copy-start(f32[16,8,6]{1,2,0:T(8,128)S(1)} %get-tuple-element.11) | copy-start | bytes 9220
  480.5 23.5 %copy-start.25 = (f32[16,8,6]{1,2,0:T(8,128)}, f32[16,8,6]{1,2,0:T(8,128)S(1)}, u32[]{:S(2)}) copy-start(f32[16,8,6]{1,2,0:T(8,128)S(1)} %get-tuple-element.12) | copy-start | bytes 9220
  487.5 16.5 %all-to-all-start.9 = ((f32[32,1,8,1,6]{2,3,4,1,0:T(1,128)}), f32[32,1,8,1,6]{2,3,4,1,0:T(1,128)}, u32[]{:S(2)}, u32[]{:S(2)}) async-start(f32[32,1,8,1,6]{2,3,4,1,0:T(1,128)} %copy.794), calls=%async_computation.9 | async-start | bytes 196608 | tf_op jit(solution)/shard_map/all_to_all | solution.py:176
  504.0 35.8 %all-to-all-start.2 = ((f32[32,1,8,1,384]{4,2,3,1,0:T(8,128)}), f32[32,1,8,1,384]{4,2,3,1,0:T(8,128)S(1)}, u32[]{:S(2)}, u32[]{:S(2)}) async-start(f32[32,1,8,1,384]{4,2,3,1,0:T(8,128)} %get-tuple-element.99), calls=%async_computation.2 | async-start | bytes 786432 | tf_op jit(solution)/shard_map/all_to_all | solution.py:189
  539.8 22.4 %all-to-all-start.5 = ((f32[32,1,8,1,384]{4,2,3,1,0:T(8,128)}), f32[32,1,8,1,384]{4,2,3,1,0:T(8,128)}, u32[]{:S(2)}, u32[]{:S(2)}) async-start(f32[32,1,8,1,384]{4,2,3,1,0:T(8,128)} %get-tuple-element.97), calls=%async_computation.5 | async-start | bytes 786432 | tf_op jit(solution)/shard_map/all_to_all | solution.py:189
  562.2 28.9 %all-to-all-start.11 = ((f32[32,1,8,1,384]{4,2,3,1,0:T(8,128)}), f32[32,1,8,1,384]{4,2,3,1,0:T(8,128)S(1)}, u32[]{:S(2)}, u32[]{:S(2)}) async-start(f32[32,1,8,1,384]{4,2,3,1,0:T(8,128)} %get-tuple-element.98), calls=%async_computation.11 | async-start | bytes 786432 | tf_op jit(solution)/shard_map/all_to_all | solution.py:189
  591.1 24.5 %all-to-all-start.8 = ((f32[32,1,8,1,384]{4,2,3,1,0:T(8,128)}), f32[32,1,8,1,384]{4,2,3,1,0:T(8,128)}, u32[]{:S(2)}, u32[]{:S(2)}) async-start(f32[32,1,8,1,384]{4,2,3,1,0:T(8,128)} %get-tuple-element.96), calls=%async_computation.8 | async-start | bytes 786432 | tf_op jit(solution)/shard_map/all_to_all | solution.py:189
  600.5 119.7 %all-reduce.3.cloned.1.call-start = ((), (), s32[]{:S(2)}) async-start(), calls=%async_computation.21 | async-start | bytes 6291456 | tf_op jit(solution)/shard_map/psum | solution.py:238
  631.5 91.7 %copy-start.75 = (f32[1536]{0:T(1024)S(1)}, f32[1536]{0:T(1024)}, u32[]{:S(2)}) copy-start(f32[1536]{0:T(1024)} %param.32) | copy-start | bytes 18436
  631.5 139.1 %all-gather.21.cloned.1.call-start = ((), (), s32[]{:S(2)}) async-start(), calls=%async_computation.17 | async-start | bytes 3932160 | tf_op jit(solution)/shard_map/all_gather | solution.py:245
  731.6 79.4 %all-gather.25.cloned.1.call-start = ((), (), s32[]{:S(2)}) async-start(), calls=%async_computation.19 | async-start | bytes 3932160 | tf_op jit(solution)/shard_map/all_gather | solution.py:245
  739.1 112.2 %all-gather.23.cloned.1.call-start = ((), (), s32[]{:S(2)}) async-start(), calls=%async_computation.18 | async-start | bytes 3932160 | tf_op jit(solution)/shard_map/all_gather | solution.py:245
  747.0 144.7 %all-gather.27.cloned.1.call-start = ((), (), s32[]{:S(2)}) async-start(), calls=%async_computation.20 | async-start | bytes 3932160 | tf_op jit(solution)/shard_map/all_gather | solution.py:245
  (65 other events, 363.4 us)
Sparse Core Ops, SparseCore 0:
  15.2 77.4 all-gather.16
  95.7 74.0 all-gather.14
  172.8 74.0 all-gather.18
  249.7 74.0 all-gather.12
  631.6 88.5 all-reduce.2
  731.7 38.8 all-gather.20
  772.2 38.6 all-gather.24
  812.6 38.6 all-gather.22
  853.0 38.6 all-gather.26
